TPU v7x, 256 devices: a whole 4x4x8 slice. The times are simulated.
256 devices in a mesh: pop: 32 (over x_lo, z, core), tp: 8 (over x_hi, y).
Axes of the slice: x: 4 (x_hi: 2, x_lo: 2; x = x_hi * 2 + x_lo), y: 4, z: 8, core: 2. Of those that a mesh axis runs over, the one named last changes fastest.
Arguments:
- hidden: bfloat16 [2048, 5120], P('pop', 'tp'), may hold values from -24 to 24
- norm_gain: float32 [5120], P('tp'), may hold values from 0.25 to 1.75
- right_factors: bfloat16 [5120, 128], P('tp'), may hold values from -0.078125 to 0.078125
- left_factors: bfloat16 [77824, 128], P(('pop', 'tp')), may hold values from -4 to 4
- targets: int32 [2048], replicated, may hold values from 0 to 77823
- master: float32 [77824, 5120], P(('pop', 'tp')), may hold values from -0.2934839 to 0.2934839
Outputs:
- member_loglik: float32 [64], replicated
- new_master: float32 [77824, 5120], P(('pop', 'tp'))
All inputs are finite; a program needn't handle non-finite values.
Results may differ from a plain program's by a relative error of at most 0.0026.
The roundings to bfloat16 on the way count: a program that leaves them out, or rounds other values in their place, can miss the bound.
Values may be sent and summed in bfloat16 or wider, within the bound.
A program may use at most 128 MiB of HBM per device.

v0:
```python
import jax
import jax.numpy as jnp
from jax import lax
from jax.sharding import PartitionSpec as P

D = 5120
RANK = 4
SEQ = 32
NORM_EPS = 1e-06
SIGMA_NOISE = 0.25
LEARN_RATE = 0.5


def contract(left, right):
    return lax.dot_general(
        left, right, (((1,), (1,)), ((), ())), preferred_element_type=jnp.float32
    )


def body(hidden, norm_gain, right_factors, left_factors, targets, master):
    tok_rows = hidden.shape[0]
    half_rows = tok_rows // 2
    fact_cols = right_factors.shape[1]
    voc_rows = master.shape[0]
    pop_index = lax.axis_index("pop")
    values = hidden.astype(jnp.float32)
    squares = lax.psum(jnp.sum(values * values, axis=1), "tp")
    row_scale = lax.rsqrt(squares / D + NORM_EPS)
    normed = (values * row_scale[:, None] * norm_gain[None, :]).astype(jnp.bfloat16)
    pair_cols = lax.dynamic_slice_in_dim(right_factors, pop_index * RANK, RANK, 1)
    partial_proj = jnp.dot(normed, pair_cols, preferred_element_type=jnp.float32)
    projection = lax.psum(partial_proj, "tp")
    member_sign = jnp.where(jnp.arange(tok_rows) < half_rows, SIGMA_NOISE, -SIGMA_NOISE).astype(
        jnp.float32
    )
    scaled = projection * member_sign[:, None]
    own_block = (lax.iota(jnp.int32, fact_cols) // RANK == pop_index).astype(jnp.float32)
    lowrank = (jnp.tile(scaled, (1, fact_cols // RANK)) * own_block[None, :]).astype(jnp.bfloat16)
    head = master.astype(jnp.bfloat16)
    full_rows, full_right = (
        lax.all_gather(normed, "tp", axis=1, tiled=True),
        lax.all_gather(right_factors, "tp", axis=0, tiled=True),
    )
    joined_rows = jnp.concatenate([full_rows, lowrank], axis=1)
    piece = lax.all_gather(joined_rows, "pop", axis=0, tiled=True)
    logits = contract(piece[:, :D], head) + contract(piece[:, D:], left_factors)
    offset = (pop_index * lax.axis_size("tp") + lax.axis_index("tp")) * voc_rows
    row_max = jnp.max(logits, axis=1)
    column_ids = lax.iota(jnp.int32, voc_rows)
    target_logit = jnp.sum(
        jnp.where(offset + column_ids[None, :] == targets[:, None], logits, 0.0), axis=1
    )
    all_max = lax.pmax(row_max, ("pop", "tp"))
    row_sum = jnp.sum(jnp.exp(logits - all_max[:, None]), axis=1)
    all_sum, all_target = lax.psum((row_sum, target_logit), ("pop", "tp"))
    logprob = all_target - all_max - jnp.log(all_sum)
    member_loglik = jnp.mean(logprob.reshape(-1, SEQ), axis=1)
    fitness = member_loglik[0::2] - member_loglik[1::2]
    weight_cols = jnp.repeat(fitness, RANK)
    scaled_left = (left_factors.astype(jnp.float32) * weight_cols[None, :]).astype(jnp.bfloat16)
    update = contract(scaled_left, full_right)
    new_master = master + LEARN_RATE * update
    return (member_loglik, new_master)


def solution(mesh):
    in_specs = (
        P("pop", "tp"),
        P("tp"),
        P("tp", None),
        P(("pop", "tp"), None),
        P(),
        P(("pop", "tp"), None),
    )
    out_specs = (P(), P(("pop", "tp"), None))
    return jax.shard_map(body, mesh=mesh, in_specs=in_specs, out_specs=out_specs, check_vma=False)
```

profile of v0, /device:TPU:1, one launch (start us, length us, event | category | flops | bytes accessed | tf_op | source)
XLA Modules:
  0.0 395.4 jit_solution(13763955117740881840)
XLA Ops:
  7.2 0.0 copy-start
  7.2 0.0 all-gather.3.cloned.1.call-start
  7.3 1.0 fusion.11
  8.3 21.5 %psum.28 = f32[64]{0:T(128)S(1)} all-reduce(f32[64]{0:T(128)S(1)} %fusion.11), channel_id=1, replica_groups=mesh['pop'=32,'tp'=8] {'tp'}, use_global_device_ids=true, to_apply=%region_1.0 | all-reduce | flops 64 | bytes 512 | tf_op jit(solution)/shard_map/psum | solution.py:27
  29.8 1.0 fusion.13
  30.8 29.9 %all_gather.9 = bf16[64,5120]{1,0:T(8,128)(2,1)S(1)} all-gather(bf16[64,640]{1,0:T(8,128)(2,1)S(1)} %fusion.13), channel_id=1, replica_groups=mesh['pop'=32,'tp'=8] {'tp'}, dimensions={1}, use_global_device_ids=true | all-gather | bytes 737280 | tf_op jit(solution)/shard_map/all_gather | solution.py:41
  60.7 1.2 fusion.14
  61.8 15.7 %psum.29 = f32[64,4]{0,1:T(4,128)S(1)} all-reduce(f32[64,4]{0,1:T(4,128)S(1)} %fusion.14), channel_id=1, replica_groups=mesh['pop'=32,'tp'=8] {'tp'}, use_global_device_ids=true, to_apply=%region_2.0 | all-reduce | flops 256 | bytes 2048 | tf_op jit(solution)/shard_map/psum | solution.py:32
  77.6 0.1 multiply_convert_fusion.2
  77.7 0.1 copy.9
  77.8 0.9 pad_maximum_fusion
  78.7 0.0 all-gather.3.cloned.1.call-update
  78.7 0.0 all-gather.5.cloned.1.call-start
  78.7 0.7 all-gather.5.cloned.1.call-update
  79.5 135.6 %all-gather.3.cloned.1.call-done = bf16[2048,5248]{1,0:T(8,128)(2,1)} async-done(((bf16[64,5248]{1,0:T(8,128)(2,1)}), bf16[2048,5248]{1,0:T(8,128)(2,1)}) %all-gather.3.cloned.1.call-update) | async-done | bytes 21495824 | tf_op jit(solution)/shard_map/all_gather | solution.py:45
  215.0 0.0 copy-done
  215.0 1.5 fusion.9
  216.6 0.0 copy-start.1
  216.6 12.6 %fusion.18 = (f32[2048]{0:T(1024)S(1)}, f32[2048,304]{0,1:T(8,128)S(1)}) fusion(f32[2048,304]{0,1:T(8,128)S(1)} %fusion.9, f32[304,5120]{1,0:T(8,128)} %param.11, bf16[2048,5248]{1,0:T(8,128)(2,1)} %all-gather.3.cloned.1.call-done), kind=kOutput, calls=%fused_computation.33 | convolution fusion | flops 6378141696 | bytes 32186368 | tf_op jit(solution)/shard_map/dot_general | solution.py:15
  229.2 78.5 %pmax.7 = f32[2048]{0:T(1024)S(1)} all-reduce(f32[2048]{0:T(1024)S(1)} %get-tuple-element.6), channel_id=1, replica_groups=mesh['pop'=32,'tp'=8] {'pop','tp'}, use_global_device_ids=true, to_apply=%region_6.7 | all-reduce | flops 2048 | bytes 16384 | tf_op jit(solution)/shard_map/pmax | solution.py:53
  307.8 0.0 copy-done.1
  307.8 0.6 select_reduce_fusion
  308.4 72.7 %all-reduce = (f32[2048]{0:T(1024)S(1)}, f32[2048]{0:T(1024)S(1)}) all-reduce(f32[2048]{0:T(1024)S(1)} %get-tuple-element.3, f32[2048]{0:T(1024)S(1)} %get-tuple-element.2), channel_id=1, replica_groups=mesh['pop'=32,'tp'=8] {'pop','tp'}, use_global_device_ids=true, to_apply=%region_8.9 | all-reduce | flops 4096 | bytes 32768 | tf_op jit(solution)/shard_map/psum | solution.py:55
  381.1 0.1 reshape.41
  381.1 0.1 reduce_sum.39
  381.3 0.0 copy-start.2
  381.3 0.1 slice.14
  381.4 0.1 slice.15
  381.5 0.1 broadcast_in_dim.25
  381.6 0.1 mul.72
  381.7 0.0 all-gather.5.cloned.1.call-done
  381.7 6.8 %fusion.2 = f32[304,5120]{1,0:T(8,128)} fusion(f32[304,5120]{1,0:T(8,128)} %param.11, bf16[5120,128]{1,0:T(8,128)(2,1)} %all-gather.5.cloned.1.call-done, bf16[304,128]{1,0:T(8,128)(2,1)S(1)} %copy-done, f32[128]{0:T(128)S(1)} %mul.72), kind=kOutput, calls=%fused_computation.3 | convolution fusion | flops 401688576 | bytes 13840896 | tf_op jit(solution)/shard_map/dot_general | solution.py:15
  388.6 0.0 copy-done.2
  (9 shorter events, 0.1 us)
Async XLA Ops:
  7.2 207.9 %copy-start = (bf16[304,128]{1,0:T(8,128)(2,1)S(1)}, bf16[304,128]{1,0:T(8,128)(2,1)}, u32[]{:S(2)}) copy-start(bf16[304,128]{1,0:T(8,128)(2,1)} %param.9) | copy-start | bytes 233476
  7.2 207.9 %all-gather.3.cloned.1.call-start = ((), (), s32[]{:S(2)}) async-start(), calls=%async_computation | async-start | bytes 22167552 | tf_op jit(solution)/shard_map/all_gather | solution.py:45
  78.7 303.1 %all-gather.5.cloned.1.call-start = ((), (), s32[]{:S(2)}) async-start(), calls=%async_computation.1 | async-start | bytes 1474560 | tf_op jit(solution)/shard_map/all_gather | solution.py:42
  216.6 91.2 %copy-start.1 = (s32[2048]{0:T(1024)S(1)}, s32[2048]{0:T(1024)}, u32[]{:S(2)}) copy-start(s32[2048]{0:T(1024)} %param.10) | copy-start | bytes 24580
  381.3 7.3 %copy-start.2 = (f32[64]{0:T(128)}, f32[64]{0:T(128)S(1)}, u32[]{:S(2)}) copy-start(f32[64]{0:T(128)S(1)} %broadcast_multiply_fusion.1) | copy-start | bytes 772
Sparse Core Ops, SparseCore 0:
  78.8 136.1 all-gather.2
  217.6 52.0 all-gather.4
where the time goes:
time: 396 us; the launch traced here: 395 us
  blocking collectives  218 us (55%)
  waiting for transfers between devices  136 us (34%)
  matrix products  22.2 us (6%)
  between operations  14.2 us (4%)
    all_gather x1, waiting for transfers between devices, body(): piece = lax.all_gather(joined_rows, 'pop', axis=0, tiled=True)  136 us
    pmax x1, blocking collectives, body(): all_max = lax.pmax(row_max, ('pop', 'tp'))  78.5 us
    psum x1, blocking collectives, body(): all_sum, all_target = lax.psum((row_sum, target_logit), ('pop', 'tp'))  72.7 us
    all_gather x1, blocking collectives, body(): lax.all_gather(normed, 'tp', axis=1, tiled=True)  29.9 us
    psum x1, blocking collectives, body(): squares = lax.psum(jnp.sum(values * values, axis=1), 'tp')  21.5 us
    dot_general x3, matrix products, contract(): lax.dot_general(left, right, (((1,), (1,)), ((), ())), preferred_element_...  21 us
    psum x1, blocking collectives, body(): projection = lax.psum(partial_proj, 'tp')  15.7 us
  transfers between devices with their start and end apart: 2, of which 1 were waited for; matrix products, arithmetic and copies ran while one was open for 4% of the time, Pallas kernels for 0%

commit v1 on v0

--- a/solution.py
+++ b/solution.py
@@ -52,7 +52,7 @@
     )
     all_max = lax.pmax(row_max, ("pop", "tp"))
     row_sum = jnp.sum(jnp.exp(logits - all_max[:, None]), axis=1)
-    all_sum, all_target = lax.psum((row_sum, target_logit), ("pop", "tp"))
+    all_sum, all_target = lax.psum(lax.psum((row_sum, target_logit), "pop"), "tp")
     logprob = all_target - all_max - jnp.log(all_sum)
     member_loglik = jnp.mean(logprob.reshape(-1, SEQ), axis=1)
     fitness = member_loglik[0::2] - member_loglik[1::2]

time: 396 us -> 465 us (1.17)
  the two profiles are of different devices: /device:TPU:1 before, /device:TPU:6 now
where the time goes in v1:
time: 465 us
  blocking collectives  299 us (64%)
  waiting for transfers between devices  125 us (27%)
  matrix products  22.2 us (5%)
  between operations  14.2 us (3%)
    all_gather x1, waiting for transfers between devices, body(): piece = lax.all_gather(joined_rows, 'pop', axis=0, tiled=True)  124 us
    psum x1, blocking collectives, body(): lax.psum((row_sum, target_logit), 'pop')  106 us
    pmax x1, blocking collectives, body(): all_max = lax.pmax(row_max, ('pop', 'tp'))  77 us
    psum x1, blocking collectives, body(): lax.psum(lax.psum((row_sum, target_logit), 'pop'), 'tp')  39.3 us
    all_gather x1, blocking collectives, body(): lax.all_gather(normed, 'tp', axis=1, tiled=True)  35.2 us
    psum x1, blocking collectives, body(): squares = lax.psum(jnp.sum(values * values, axis=1), 'tp')  22.8 us
    dot_general x3, matrix products, contract(): lax.dot_general(left, right, (((1,), (1,)), ((), ())), preferred_element_...  21 us
    psum x1, blocking collectives, body(): projection = lax.psum(partial_proj, 'tp')  19.3 us
  transfers between devices with their start and end apart: 2, of which 1 were waited for; matrix products, arithmetic and copies ran while one was open for 3% of the time, Pallas kernels for 0%

profile of v1, /device:TPU:6, one launch (start us, length us, event | category | flops | bytes accessed | tf_op | source)
XLA Modules:
  0.0 464.8 jit_solution(401056864205948864)
XLA Ops:
  7.2 0.0 copy-start
  7.2 0.0 all-gather.3.cloned.1.call-start
  7.3 1.0 fusion.11
  8.3 22.8 %psum.42 = f32[64]{0:T(128)S(1)} all-reduce(f32[64]{0:T(128)S(1)} %fusion.11), channel_id=1, replica_groups=mesh['pop'=32,'tp'=8] {'tp'}, use_global_device_ids=true, to_apply=%region_1.0 | all-reduce | flops 64 | bytes 512 | tf_op jit(solution)/shard_map/psum | solution.py:27
  31.1 1.0 fusion.13
  32.1 35.2 %all_gather.9 = bf16[64,5120]{1,0:T(8,128)(2,1)S(1)} all-gather(bf16[64,640]{1,0:T(8,128)(2,1)S(1)} %fusion.13), channel_id=1, replica_groups=mesh['pop'=32,'tp'=8] {'tp'}, dimensions={1}, use_global_device_ids=true | all-gather | bytes 737280 | tf_op jit(solution)/shard_map/all_gather | solution.py:41
  67.3 1.2 fusion.14
  68.5 19.3 %psum.43 = f32[64,4]{0,1:T(4,128)S(1)} all-reduce(f32[64,4]{0,1:T(4,128)S(1)} %fusion.14), channel_id=1, replica_groups=mesh['pop'=32,'tp'=8] {'tp'}, use_global_device_ids=true, to_apply=%region_2.0 | all-reduce | flops 256 | bytes 2048 | tf_op jit(solution)/shard_map/psum | solution.py:32
  87.9 0.1 multiply_convert_fusion.2
  88.0 0.1 copy.9
  88.0 0.9 pad_maximum_fusion
  88.9 0.0 all-gather.3.cloned.1.call-update
  89.0 0.0 all-gather.5.cloned.1.call-start
  89.0 0.7 all-gather.5.cloned.1.call-update
  89.7 123.9 %all-gather.3.cloned.1.call-done = bf16[2048,5248]{1,0:T(8,128)(2,1)} async-done(((bf16[64,5248]{1,0:T(8,128)(2,1)}), bf16[2048,5248]{1,0:T(8,128)(2,1)}) %all-gather.3.cloned.1.call-update) | async-done | bytes 21495824 | tf_op jit(solution)/shard_map/all_gather | solution.py:45
  213.6 0.0 copy-done
  213.6 1.5 fusion.9
  215.1 0.0 copy-start.1
  215.2 12.7 %fusion.18 = (f32[2048]{0:T(1024)S(1)}, f32[2048,304]{0,1:T(8,128)S(1)}) fusion(f32[2048,304]{0,1:T(8,128)S(1)} %fusion.9, f32[304,5120]{1,0:T(8,128)} %param.11, bf16[2048,5248]{1,0:T(8,128)(2,1)} %all-gather.3.cloned.1.call-done), kind=kOutput, calls=%fused_computation.33 | convolution fusion | flops 6378141696 | bytes 32186368 | tf_op jit(solution)/shard_map/dot_general | solution.py:15
  227.8 77.0 %pmax.7 = f32[2048]{0:T(1024)S(1)} all-reduce(f32[2048]{0:T(1024)S(1)} %get-tuple-element.8), channel_id=1, replica_groups=mesh['pop'=32,'tp'=8] {'pop','tp'}, use_global_device_ids=true, to_apply=%region_7.8 | all-reduce | flops 2048 | bytes 16384 | tf_op jit(solution)/shard_map/pmax | solution.py:53
  304.8 0.0 copy-done.1
  304.8 0.6 select_reduce_fusion
  305.4 105.8 %all-reduce = (f32[2048]{0:T(1024)S(1)}, f32[2048]{0:T(1024)S(1)}) all-reduce(f32[2048]{0:T(1024)S(1)} %get-tuple-element.3, f32[2048]{0:T(1024)S(1)} %get-tuple-element.2), channel_id=1, replica_groups=mesh['pop'=32,'tp'=8] {'pop'}, use_global_device_ids=true, to_apply=%region_9.10 | all-reduce | flops 4096 | bytes 32768 | tf_op jit(solution)/shard_map/psum | solution.py:55
  411.2 39.3 %all-reduce.1 = (f32[2048]{0:T(1024)S(1)}, f32[2048]{0:T(1024)S(1)}) all-reduce(f32[2048]{0:T(1024)S(1)} %get-tuple-element.4, f32[2048]{0:T(1024)S(1)} %get-tuple-element.5), channel_id=1, replica_groups=mesh['pop'=32,'tp'=8] {'tp'}, use_global_device_ids=true, to_apply=%region_10.11 | all-reduce | flops 4096 | bytes 32768 | tf_op jit(solution)/shard_map/psum | solution.py:55
  450.5 0.1 reshape.41
  450.5 0.1 reduce_sum.39
  450.7 0.0 copy-start.2
  450.7 0.1 slice.14
  450.8 0.1 slice.15
  450.9 0.1 broadcast_in_dim.25
  451.0 0.1 mul.72
  451.1 0.0 all-gather.5.cloned.1.call-done
  451.2 6.8 %fusion.2 = f32[304,5120]{1,0:T(8,128)} fusion(f32[304,5120]{1,0:T(8,128)} %param.11, bf16[5120,128]{1,0:T(8,128)(2,1)} %all-gather.5.cloned.1.call-done, bf16[304,128]{1,0:T(8,128)(2,1)S(1)} %copy-done, f32[128]{0:T(128)S(1)} %mul.72), kind=kOutput, calls=%fused_computation.3 | convolution fusion | flops 401688576 | bytes 13840896 | tf_op jit(solution)/shard_map/dot_general | solution.py:15
  458.0 0.0 copy-done.2
  (9 shorter events, 0.1 us)
Async XLA Ops:
  7.2 206.5 %copy-start = (bf16[304,128]{1,0:T(8,128)(2,1)S(1)}, bf16[304,128]{1,0:T(8,128)(2,1)}, u32[]{:S(2)}) copy-start(bf16[304,128]{1,0:T(8,128)(2,1)} %param.9) | copy-start | bytes 233476
  7.2 206.4 %all-gather.3.cloned.1.call-start = ((), (), s32[]{:S(2)}) async-start(), calls=%async_computation | async-start | bytes 22167552 | tf_op jit(solution)/shard_map/all_gather | solution.py:45
  89.0 362.2 %all-gather.5.cloned.1.call-start = ((), (), s32[]{:S(2)}) async-start(), calls=%async_computation.1 | async-start | bytes 1474560 | tf_op jit(solution)/shard_map/all_gather | solution.py:42
  215.1 89.6 %copy-start.1 = (s32[2048]{0:T(1024)S(1)}, s32[2048]{0:T(1024)}, u32[]{:S(2)}) copy-start(s32[2048]{0:T(1024)} %param.10) | copy-start | bytes 24580
  450.7 7.3 %copy-start.2 = (f32[64]{0:T(128)}, f32[64]{0:T(128)S(1)}, u32[]{:S(2)}) copy-start(f32[64]{0:T(128)S(1)} %broadcast_multiply_fusion.1) | copy-start | bytes 772
Sparse Core Ops, SparseCore 0:
  89.1 124.4 all-gather.2
  216.2 51.9 all-gather.4
